TPU v7x, 32 devices: a whole 2x2x4 slice. The times are simulated.
32 devices in a mesh: pb: 2 (over x), row: 16 (over z, y, core).
Axes of the slice: x: 2, y: 2, z: 4, core: 2. Of those that a mesh axis runs over, the one named last changes fastest.
Arguments:
- force_constants: float32 [9, 4608, 4608], P(None, 'row', 'pb'), may hold values from -0.1 to 3.6, as said below
- offsets: int32 [9, 3], replicated, may hold values from -2 to 2, as said below
- qpoints: int32 [2, 3], replicated, may hold values from 0 to 7
- lower_bound: float32 [2], P('pb'), may hold values from 1.5 to 2.5
- upper_bound: float32 [2], P('pb'), may hold values from 5.5 to 6.5
- start_vectors: float32 [4608, 128], P('row'), may hold values from -6 to 6
Outputs:
- basis: float32 [2, 4608, 128], P('pb', 'row')
- ritz: float32 [2, 64, 128], P('pb')
Inputs may be any that keep to these rules, and one draw needn't show every extreme that they name: `force_constants`: cell 0 is symmetric; for 1 <= c <= 4, cell c + 4 is the transpose of cell c, so every D(q) is Hermitian. `offsets`: row 0 is zero; for 1 <= c <= 4, row c + 4 is the negative of row c.
All inputs are finite; a program needn't handle non-finite values.
Results may differ from a plain program's by a relative error of at most 0.00025.
Values sent between devices are 32-bit elements; how exact they have to be, the bound alone decides.
A program may use at most 128 MiB of HBM per device.

v0:
```python
import math

import jax
import jax.numpy as jnp
from jax import lax
from jax.sharding import PartitionSpec as P

MODES = 4608
QDEN = 8


highest = lax.Precision.HIGHEST


def product(left, right):
    return jnp.dot(left, right, precision=highest, preferred_element_type=jnp.float32)


def inner_product(left, right):
    return lax.dot_general(
        left, right, (((0,), (0,)), ((), ())), precision=highest, preferred_element_type=jnp.float32
    )


def complex_times(left_real, left_imag, right_real, right_imag):
    return (
        product(left_real, right_real) - product(left_imag, right_imag),
        product(left_real, right_imag) + product(left_imag, right_real),
    )


def phase_table(qpoints, offsets):
    turns = jnp.sum(qpoints[:, None, :] * offsets[None, :, :], axis=2)
    turns = jnp.mod(turns, QDEN)
    angle = 2.0 * math.pi / QDEN * turns.astype(jnp.float32)
    return jnp.stack([jnp.cos(angle), jnp.sin(angle)], axis=1)


def factor_inverse(gram_real, gram_imag):
    order_size = gram_real.shape[0]
    embedded = jnp.stack(
        [jnp.stack([gram_real, -gram_imag], axis=2), jnp.stack([gram_imag, gram_real], axis=2)],
        axis=1,
    ).reshape(2 * order_size, 2 * order_size)
    lower_factor = jnp.linalg.cholesky(embedded)
    identity = jnp.eye(2 * order_size, dtype=gram_real.dtype)
    inverse = jax.scipy.linalg.solve_triangular(lower_factor, identity, lower=True)
    blocks = inverse.reshape(order_size, 2, order_size, 2)
    return (blocks[:, 0, :, 0], blocks[:, 1, :, 0])


def right_block(inverse_real, inverse_imag):
    upper_half = jnp.concatenate([inverse_real.T, -inverse_imag.T], axis=1)
    lower_half = jnp.concatenate([inverse_imag.T, inverse_real.T], axis=1)
    return jnp.concatenate([upper_half, lower_half], axis=0)


def split_gram(matrix, vector_count):
    return (
        matrix[:vector_count, :vector_count] + matrix[vector_count:, vector_count:],
        matrix[:vector_count, vector_count:] - matrix[vector_count:, :vector_count],
    )


def combine_parts(part_real, part_imag, vector_count):
    return jnp.concatenate(
        [
            part_real[:, :vector_count] - part_imag[:, vector_count:],
            part_real[:, vector_count:] + part_imag[:, :vector_count],
        ],
        axis=1,
    )


def chebyshev(vectors, apply_matrix, lower_value, upper_value, first_image):
    centre = 0.5 * (upper_value + lower_value)
    spread = 0.5 * (upper_value - lower_value)
    previous = vectors
    first_image = apply_matrix(vectors)
    current = (first_image - centre * vectors) / spread
    following = 2.0 * (apply_matrix(current) - centre * current) / spread - previous
    previous, current = (current, following)
    return current


def on_device(force_constants, offsets, qpoints, lower_bound, upper_bound, start_vectors):
    cell_count, row_count, col_count = force_constants.shape
    qcount = qpoints.shape[0]
    vector_count = start_vectors.shape[1] // 2
    coefficients = phase_table(qpoints, offsets).reshape(2 * qcount, cell_count)
    partial_value = product(
        coefficients, force_constants.reshape(cell_count, row_count * col_count)
    )
    partial_value = partial_value.reshape(qcount, 2, row_count, col_count)
    owned_block = lax.all_to_all(partial_value, "pb", split_axis=0, concat_axis=3, tiled=True)
    dyn_real = owned_block[0, 0]
    dyn_imag = owned_block[0, 1]

    def accumulate(piece):
        return combine_parts(product(dyn_real, piece), product(dyn_imag, piece), vector_count)

    def apply_matrix(vectors):
        return accumulate(lax.all_gather(vectors, "row", axis=0, tiled=True))

    lower_value = lower_bound[0]
    upper_value = upper_bound[0]
    first_pass = chebyshev(start_vectors, apply_matrix, lower_value, upper_value, None)
    final_pass = chebyshev(first_pass, apply_matrix, lower_value, upper_value, None)
    image = apply_matrix(final_pass)
    over_total, proj_total = lax.psum(
        (inner_product(final_pass, final_pass), inner_product(final_pass, image)), "row"
    )
    over_real, over_imag = split_gram(over_total, vector_count)
    proj_real, proj_imag = split_gram(proj_total, vector_count)
    inverse_real, inverse_imag = factor_inverse(over_real, over_imag)
    basis_local = math.sqrt(MODES) * product(final_pass, right_block(inverse_real, inverse_imag))
    temp_real, temp_imag = complex_times(proj_real, proj_imag, inverse_real.T, -inverse_imag.T)
    ritz_real, ritz_imag = complex_times(inverse_real, inverse_imag, temp_real, temp_imag)
    ritz_local = jnp.concatenate([ritz_real, ritz_imag], axis=1)
    return (basis_local[None], ritz_local[None])


def solution(mesh):
    return jax.shard_map(
        on_device,
        mesh=mesh,
        in_specs=(P(None, "row", "pb"), P(), P(), P("pb"), P("pb"), P("row", None)),
        out_specs=(P("pb", "row", None), P("pb", None, None)),
        check_vma=False,
    )
```

profile of v0, /device:TPU:0, one launch (start us, length us, event | category | flops | bytes accessed | tf_op | source)
XLA Modules:
  0.0 597.8 jit_solution(8227221269217695793)
XLA Ops:
  7.2 0.8 copy.26
  7.9 0.8 multiply_reduce_fusion
  8.8 9.7 %slice_bitcast_fusion = f32[288,2304,9]{1,0,2:T(8,128)S(1)} fusion(f32[9,288,2304]{2,1,0:T(8,128)} %param.6), kind=kLoop, calls=%fused_computation.3 | loop fusion | bytes 47775744 | tf_op jit(solution)/shard_map/dot_general | solution.py:16
  18.5 51.9 %fusion = f32[2,2,288,2304]{3,1,2,0:T(2,128)} fusion(f32[288,2304,9]{1,0,2:T(8,128)S(1)} %slice_bitcast_fusion, f32[2,1,9]{2,1,0:T(1,128)S(1)} %sin.10, f32[2,1,9]{2,1,0:T(1,128)S(1)} %get-tuple-element.4), kind=kOutput, calls=%fused_computation | convolution fusion | flops 286654496 | bytes 34504848 | tf_op jit(solution)/shard_map/dot_general | solution.py:16
  70.4 7.7 %all-to-all-start = ((f32[2,2,288,2304]{3,1,2,0:T(2,128)}), f32[2,2,288,2304]{3,1,2,0:T(2,128)}, u32[]{:S(2)}, u32[]{:S(2)}) async-start(f32[2,2,288,2304]{3,1,2,0:T(2,128)} %fusion), calls=%async_computation | async-start | bytes 21233664 | tf_op jit(solution)/shard_map/all_to_all | solution.py:95
  78.2 0.7 all-gather.6.cloned.1.call-update
  78.9 0.3 all-gather.8.cloned.1.call-start
  80.5 115.4 %all-to-all-done = f32[2,2,288,2304]{3,1,2,0:T(2,128)} async-done(((f32[2,2,288,2304]{3,1,2,0:T(2,128)}), f32[2,2,288,2304]{3,1,2,0:T(2,128)}, u32[]{:S(2)}, u32[]{:S(2)}) %all-to-all-start) | async-done | bytes 10616864 | tf_op jit(solution)/shard_map/all_to_all | solution.py:95
  195.9 16.3 %copy.31 = f32[1,2,288,2,2304]{4,3,2,1,0:T(2,128)} copy(f32[1,2,288,2,2304]{4,1,2,3,0:T(2,128)} %bitcast.9) | data formatting | bytes 21233664 | tf_op jit(solution)/shard_map/all_to_all | solution.py:95
  212.2 13.9 %all_to_all.16 = f32[1,2,288,4608]{3,2,1,0:T(8,128)} reshape(f32[1,2,288,2,2304]{4,3,2,1,0:T(2,128)} %copy.31) | data formatting | bytes 21233664 | tf_op jit(solution)/shard_map/all_to_all | solution.py:95
  226.2 7.2 %fusion.7 = f32[288,128]{1,0:T(8,128)S(1)} fusion(f32[4608,128]{1,0:T(8,128)} %all-gather.6.cloned.1.call-done, f32[1,2,288,4608]{3,2,1,0:T(8,128)} %all_to_all.16), kind=kOutput, calls=%fused_computation.10 | convolution fusion | flops 2038431744 | bytes 7815168 | tf_op jit(solution)/shard_map/dot_general | solution.py:16
  233.4 6.4 %fusion.12 = f32[288,128]{1,0:T(8,128)S(1)} fusion(f32[4608,128]{1,0:T(8,128)S(1)} %copy-done, f32[1,2,288,4608]{3,2,1,0:T(8,128)} %all_to_all.16), kind=kOutput, calls=%fused_computation.15 | convolution fusion | flops 2038431744 | bytes 7815168 | tf_op jit(solution)/shard_map/dot_general | solution.py:16
  240.0 0.8 fusion.14
  240.8 0.6 all-gather.10.cloned.1.call-start
  241.4 42.4 %all-gather.8.cloned.1.call-done = f32[4608,128]{1,0:T(8,128)} async-done(((f32[288,128]{1,0:T(8,128)}), f32[4608,128]{1,0:T(8,128)}) %all-gather.8.cloned.1.call-update) | async-done | bytes 2359312 | tf_op jit(solution)/shard_map/all_gather | solution.py:103
  283.8 7.8 %fusion.6 = f32[288,128]{1,0:T(8,128)S(1)} fusion(f32[4608,128]{1,0:T(8,128)} %all-gather.8.cloned.1.call-done, f32[1,2,288,4608]{3,2,1,0:T(8,128)} %all_to_all.16), kind=kOutput, calls=%fused_computation.9 | convolution fusion | flops 2038431744 | bytes 7815168 | tf_op jit(solution)/shard_map/dot_general | solution.py:16
  291.6 6.4 %fusion.11 = f32[288,128]{1,0:T(8,128)S(1)} fusion(f32[4608,128]{1,0:T(8,128)S(1)} %copy-done.2, f32[1,2,288,4608]{3,2,1,0:T(8,128)} %all_to_all.16), kind=kOutput, calls=%fused_computation.14 | convolution fusion | flops 2038431744 | bytes 7815168 | tf_op jit(solution)/shard_map/dot_general | solution.py:16
  298.2 0.8 fusion.17
  299.0 41.1 %all-gather.10.cloned.1.call-done = f32[4608,128]{1,0:T(8,128)} async-done(((f32[288,128]{1,0:T(8,128)}), f32[4608,128]{1,0:T(8,128)}) %all-gather.10.cloned.1.call-update) | async-done | bytes 2359312 | tf_op jit(solution)/shard_map/all_gather | solution.py:103
  340.2 7.8 %fusion.5 = f32[288,128]{1,0:T(8,128)S(1)} fusion(f32[4608,128]{1,0:T(8,128)} %all-gather.10.cloned.1.call-done, f32[1,2,288,4608]{3,2,1,0:T(8,128)} %all_to_all.16), kind=kOutput, calls=%fused_computation.8 | convolution fusion | flops 2038431744 | bytes 7815168 | tf_op jit(solution)/shard_map/dot_general | solution.py:16
  348.0 6.4 %fusion.10 = f32[288,128]{1,0:T(8,128)S(1)} fusion(f32[4608,128]{1,0:T(8,128)S(1)} %copy-done.3, f32[1,2,288,4608]{3,2,1,0:T(8,128)} %all_to_all.16), kind=kOutput, calls=%fused_computation.13 | convolution fusion | flops 2038431744 | bytes 7815168 | tf_op jit(solution)/shard_map/dot_general | solution.py:16
  354.6 0.8 fusion.18
  355.6 41.0 %all-gather.12.cloned.1.call-done = f32[4608,128]{1,0:T(8,128)} async-done(((f32[288,128]{1,0:T(8,128)}), f32[4608,128]{1,0:T(8,128)}) %all-gather.12.cloned.1.call-update) | async-done | bytes 2359312 | tf_op jit(solution)/shard_map/all_gather | solution.py:103
  396.6 7.8 %fusion.4 = f32[288,128]{1,0:T(8,128)S(1)} fusion(f32[4608,128]{1,0:T(8,128)} %all-gather.12.cloned.1.call-done, f32[1,2,288,4608]{3,2,1,0:T(8,128)} %all_to_all.16), kind=kOutput, calls=%fused_computation.7 | convolution fusion | flops 2038431744 | bytes 7815168 | tf_op jit(solution)/shard_map/dot_general | solution.py:16
  404.4 6.4 %fusion.9 = f32[288,128]{1,0:T(8,128)S(1)} fusion(f32[4608,128]{1,0:T(8,128)S(1)} %copy-done.4, f32[1,2,288,4608]{3,2,1,0:T(8,128)} %all_to_all.16), kind=kOutput, calls=%fused_computation.12 | convolution fusion | flops 2038431744 | bytes 7815168 | tf_op jit(solution)/shard_map/dot_general | solution.py:16
  410.9 0.8 fusion.21
  412.0 2.1 fusion.70
  414.1 38.9 %all-gather.14.cloned.1.call-done = f32[4608,128]{1,0:T(8,128)} async-done(((f32[288,128]{1,0:T(8,128)}), f32[4608,128]{1,0:T(8,128)}) %all-gather.14.cloned.1.call-update) | async-done | bytes 2359312 | tf_op jit(solution)/shard_map/all_gather | solution.py:103
  452.9 7.8 %fusion.3 = f32[288,128]{1,0:T(8,128)S(1)} fusion(f32[4608,128]{1,0:T(8,128)} %all-gather.14.cloned.1.call-done, f32[1,2,288,4608]{3,2,1,0:T(8,128)} %all_to_all.16), kind=kOutput, calls=%fused_computation.6 | convolution fusion | flops 2038431744 | bytes 7815168 | tf_op jit(solution)/shard_map/dot_general | solution.py:16
  460.7 6.4 %fusion.8 = f32[288,128]{1,0:T(8,128)S(1)} fusion(f32[4608,128]{1,0:T(8,128)S(1)} %copy-done.1, f32[1,2,288,4608]{3,2,1,0:T(8,128)} %all_to_all.16), kind=kOutput, calls=%fused_computation.11 | convolution fusion | flops 2038431744 | bytes 7815168 | tf_op jit(solution)/shard_map/dot_general | solution.py:16
  467.3 1.2 fusion.22
  468.7 87.1 %all-reduce.3.cloned.1.call-done = (f32[128,128]{1,0:T(8,128)}, f32[128,128]{1,0:T(8,128)}) async-done(((f32[128,128]{1,0:T(8,128)}, f32[128,128]{1,0:T(8,128)}), (f32[128,128]{1,0:T(8,128)}, f32[128,128]{1,0:T(8,128)})) %all-reduce.3.cloned.1.call-update) | async-done | bytes 131088 | tf_op jit(solution)/shard_map/psum | solution.py:110
  555.8 0.9 negate_bitcast_fusion
  556.8 2.7 copy.32
  559.5 4.2 reshape.123
  563.9 11.7 %cholesky.18 = f32[128,128]{1,0:T(8,128)S(1)} custom-call(f32[128,128]{1,0:T(8,128)S(1)} %fusion.36), custom_call_target="Cholesky" | custom-call | tf_op jit(solution)/shard_map/jit(cholesky)/cholesky | solution.py:45
  575.6 0.6 compare_reduce_fusion
  576.2 0.7 fusion.26
  576.9 9.8 %custom-call.7 = f32[1,128,128]{1,2,0:T(8,128)S(1)} custom-call(f32[1,128,128]{2,1,0:T(8,128)S(1)} %fusion.26), custom_call_target="InvertDiagBlocksLowerTriangular" | custom-call | tf_op jit(solution)/shard_map/jit(_solve_triangular)/triangular_solve | solution.py:47
  586.8 0.3 fusion.34
  587.6 0.2 convolution_subtract_fusion.1
  587.8 0.2 fusion.43
  588.1 0.2 convolution_add_fusion.1
  588.3 0.2 fusion.47
  588.6 0.2 convolution_subtract_fusion
  588.8 0.2 convolution_add_fusion
  589.1 0.7 maximum_bitcast_fusion.2
  589.8 1.0 fusion.13
  (53 shorter events, 2.3 us)
Async XLA Ops:
  70.4 125.5 %all-to-all-start = ((f32[2,2,288,2304]{3,1,2,0:T(2,128)}), f32[2,2,288,2304]{3,1,2,0:T(2,128)}, u32[]{:S(2)}, u32[]{:S(2)}) async-start(f32[2,2,288,2304]{3,1,2,0:T(2,128)} %fusion), calls=%async_computation | async-start | bytes 21233664 | tf_op jit(solution)/shard_map/all_to_all | solution.py:95
  78.1 148.0 %all-gather.6.cloned.1.call-start = ((), (), s32[]{:S(2)}) async-start(), calls=%async_computation.1 | async-start | bytes 2506752 | tf_op jit(solution)/shard_map/all_gather | solution.py:103
  78.9 204.9 %all-gather.8.cloned.1.call-start = ((), (), s32[]{:S(2)}) async-start(), calls=%async_computation.2 | async-start | bytes 2506752 | tf_op jit(solution)/shard_map/all_gather | solution.py:103
  226.2 7.2 %copy-start = (f32[4608,128]{1,0:T(8,128)S(1)}, f32[4608,128]{1,0:T(8,128)}, u32[]{:S(2)}) copy-start(f32[4608,128]{1,0:T(8,128)} %all-gather.6.cloned.1.call-done) | copy-start | bytes 7077892
  233.4 6.6 %copy-start.7 = (f32[288,128]{1,0:T(8,128)S(1)}, f32[288,128]{1,0:T(8,128)}, u32[]{:S(2)}) copy-start(f32[288,128]{1,0:T(8,128)} %param.11) | copy-start | bytes 442372
  240.8 99.4 %all-gather.10.cloned.1.call-start = ((), (), s32[]{:S(2)}) async-start(), calls=%async_computation.3 | async-start | bytes 2506752 | tf_op jit(solution)/shard_map/all_gather | solution.py:103
  283.8 7.8 %copy-start.2 = (f32[4608,128]{1,0:T(8,128)S(1)}, f32[4608,128]{1,0:T(8,128)}, u32[]{:S(2)}) copy-start(f32[4608,128]{1,0:T(8,128)} %all-gather.8.cloned.1.call-done) | copy-start | bytes 7077892
  291.6 6.6 %copy-start.9 = (f32[288,128]{1,0:T(8,128)S(1)}, f32[288,128]{1,0:T(8,128)}, u32[]{:S(2)}) copy-start(f32[288,128]{1,0:T(8,128)} %fusion.14) | copy-start | bytes 442372
  299.0 97.6 %all-gather.12.cloned.1.call-start = ((), (), s32[]{:S(2)}) async-start(), calls=%async_computation.4 | async-start | bytes 2506752 | tf_op jit(solution)/shard_map/all_gather | solution.py:103
  340.2 7.8 %copy-start.3 = (f32[4608,128]{1,0:T(8,128)S(1)}, f32[4608,128]{1,0:T(8,128)}, u32[]{:S(2)}) copy-start(f32[4608,128]{1,0:T(8,128)} %all-gather.10.cloned.1.call-done) | copy-start | bytes 7077892
  348.0 6.6 %copy-start.6 = (f32[288,128]{1,0:T(8,128)S(1)}, f32[288,128]{1,0:T(8,128)}, u32[]{:S(2)}) copy-start(f32[288,128]{1,0:T(8,128)} %fusion.17) | copy-start | bytes 442372
  355.4 97.6 %all-gather.14.cloned.1.call-start = ((), (), s32[]{:S(2)}) async-start(), calls=%async_computation.5 | async-start | bytes 2506752 | tf_op jit(solution)/shard_map/all_gather | solution.py:103
  396.6 7.8 %copy-start.4 = (f32[4608,128]{1,0:T(8,128)S(1)}, f32[4608,128]{1,0:T(8,128)}, u32[]{:S(2)}) copy-start(f32[4608,128]{1,0:T(8,128)} %all-gather.12.cloned.1.call-done) | copy-start | bytes 7077892
  404.3 6.6 %copy-start.8 = (f32[288,128]{1,0:T(8,128)S(1)}, f32[288,128]{1,0:T(8,128)}, u32[]{:S(2)}) copy-start(f32[288,128]{1,0:T(8,128)} %fusion.18) | copy-start | bytes 442372
  411.8 144.1 %all-reduce.3.cloned.1.call-start = ((), (), s32[]{:S(2)}) async-start(), calls=%async_computation.6 | async-start | bytes 262144 | tf_op jit(solution)/shard_map/psum | solution.py:110
  452.9 7.8 %copy-start.1 = (f32[4608,128]{1,0:T(8,128)S(1)}, f32[4608,128]{1,0:T(8,128)}, u32[]{:S(2)}) copy-start(f32[4608,128]{1,0:T(8,128)} %all-gather.14.cloned.1.call-done) | copy-start | bytes 7077892
  460.7 6.6 %copy-start.5 = (f32[288,128]{1,0:T(8,128)S(1)}, f32[288,128]{1,0:T(8,128)}, u32[]{:S(2)}) copy-start(f32[288,128]{1,0:T(8,128)} %fusion.21) | copy-start | bytes 442372
  555.8 31.3 %copy-start.10 = (f32[128,128]{1,0:T(8,128)S(1)}, f32[128,128]{1,0:T(8,128)}, u32[]{:S(2)}) copy-start(f32[128,128]{1,0:T(8,128)} %get-tuple-element.3) | copy-start | bytes 196612
Sparse Core Ops, SparseCore 0:
  81.2 45.3 all-gather.5
  240.9 42.8 all-gather.7
  299.1 41.0 all-gather.9
  355.5 41.0 all-gather.11
  411.9 41.0 all-gather.13
  468.7 87.1 all-reduce.2
where the time goes:
time: 607 us; the launch traced here: 598 us
  waiting for transfers between devices  367 us (60%)
  matrix products  129 us (21%)
  local copies, waits for them, and re-layouts  48.1 us (8%)
  other arithmetic  29.3 us (5%)
  between operations  16.1 us (3%)
  starting transfers between devices  8.98 us (1%)
    all_gather x5, waiting for transfers between devices, apply_matrix(): return accumulate(lax.all_gather(vectors, 'row', axis=0, tiled=True))  163 us
    dot_general x20, matrix products, product(): jnp.dot(left, right, precision=highest, preferred_element_type=jnp.float32)  125 us
    all_to_all x1, waiting for transfers between devices, on_device(): lax.all_to_all(partial_value, 'pb', split_axis=0, concat_axis=3, tiled=True)  115 us
    psum x1, waiting for transfers between devices, on_device(): lax.psum((inner_product(final_pass, final_pass), inner_product(final_pass...  87.1 us
    all_to_all x2, local copies, waits for them, and re-layouts, on_device(): lax.all_to_all(partial_value, 'pb', split_axis=0, concat_axis=3, tiled=True)  30.3 us
    another operation x4, other arithmetic, factor_inverse(): lower_factor = jnp.linalg.cholesky(embedded)  12.5 us
  transfers between devices with their start and end apart: 7, of which 6 were waited for; matrix products, arithmetic and copies ran while one was open for 3% of the time, Pallas kernels for 0%

commit v1 on v0

--- a/solution.py
+++ b/solution.py
@@ -1,8 +1,11 @@
+import functools
 import math
 
 import jax
 import jax.numpy as jnp
 from jax import lax
+from jax.experimental import pallas as pl
+from jax.experimental.pallas import tpu as pltpu
 from jax.sharding import PartitionSpec as P
 
 MODES = 4608
@@ -120,9 +123,357 @@
     return (basis_local[None], ritz_local[None])
 
 
+STEPS = 5
+MESH = pl.DeviceIdType.MESH
+
+
+def assemble_kernel(coef_ref, force_ref, high_ref, low_ref):
+    cells, tile_rows, cols = force_ref.shape
+    pairs = (cells - 1) // 2
+    points = high_ref.shape[0]
+    width = 256
+    for at in range(cols // width):
+        span = slice(at * width, (at + 1) * width)
+        home = force_ref[0, :, span]
+        real = [coef_ref[2 * q, 0] * home for q in range(points)]
+        imag = [coef_ref[2 * q + 1, 0] * home for q in range(points)]
+        for c in range(1, pairs + 1):
+            first = force_ref[c, :, span]
+            second = force_ref[c + pairs, :, span]
+            total, difference = first + second, first - second
+            for q in range(points):
+                real[q] = real[q] + coef_ref[2 * q, c] * total
+                imag[q] = imag[q] + coef_ref[2 * q + 1, c] * difference
+        for q in range(points):
+            for part, value in ((0, real[q]), (1, imag[q])):
+                high = value.astype(jnp.bfloat16)
+                high_ref[q, part, :, span] = high
+                low_ref[q, part, :, span] = (value - high.astype(jnp.float32)).astype(jnp.bfloat16)
+
+
+def assemble(coefficients, force_constants, points):
+    cells, rows, cols = force_constants.shape
+    tile = 16
+    shape = jax.ShapeDtypeStruct((points, 2, rows, cols), jnp.bfloat16)
+    block = pl.BlockSpec((points, 2, tile, cols), lambda i: (0, 0, i, 0))
+    return pl.pallas_call(
+        assemble_kernel,
+        grid=(rows // tile,),
+        out_shape=(shape, shape),
+        in_specs=[
+            pl.BlockSpec(memory_space=pltpu.SMEM),
+            pl.BlockSpec((cells, tile, cols), lambda i: (0, i, 0)),
+        ],
+        out_specs=(block, block),
+    )(coefficients, force_constants)
+
+
+def sign_row(first, second):
+    lane = lax.broadcasted_iota(jnp.int32, (1, 128), 1)
+    return jnp.where(lane < 64, first, second).astype(jnp.float32)
+
+
+def filter_kernel(
+    bounds_ref, start_ref, high_ref, low_ref, final_ref, gram_ref,
+    full, part, other, split, partner_bounds, sums, arrived,
+    send_sem, recv_sem, x_send, x_recv, b_sem, g_send, g_recv,
+):
+    p = lax.axis_index("pb")
+    row = lax.axis_index("row")
+    rows = start_ref.shape[0]
+    z, y, c = row // 4, (row // 2) % 2, row % 2
+    position = z + p * (3 - 2 * z)
+    owner = position < 2
+    not_owner = position >= 2
+    to_x = (1 - p, row)
+    to_c = (p, row + 1 - 2 * c)
+    to_y = (p, row + 2 - 4 * y)
+    to_a = (p, row + 4 - 8 * (z % 2))
+    to_b = (p, (3 - z) * 4 + y * 2 + c)
+    near, far = 1 - p, p
+    is_zero = jnp.where(position == 0, 1, 0)
+    first = near + is_zero * (far - near)
+    second = 1 - first
+    mine = (z % 2) * 4 + y * 2 + c
+
+    barrier = pltpu.get_barrier_semaphore()
+    for target in (to_x, to_c, to_y, to_a, to_b):
+        pl.semaphore_signal(barrier, inc=1, device_id=target, device_id_type=MESH)
+    pl.semaphore_wait(barrier, 5)
+
+    bound_copy = pltpu.make_async_remote_copy(
+        src_ref=bounds_ref, dst_ref=partner_bounds, send_sem=b_sem.at[0], recv_sem=b_sem.at[1],
+        device_id=to_x, device_id_type=MESH,
+    )
+    bound_copy.start()
+
+    def block_rows(index):
+        return pl.ds(pl.multiple_of(index * rows, 8), rows)
+
+    @pl.when(owner)
+    def _():
+        full[0, 0, block_rows(mine), :] = start_ref[...]
+        full[0, 1, block_rows(mine), :] = start_ref[...]
+
+    bound_copy.wait()
+
+    def send(slot, q, index, lane, target):
+        view = full.at[slot, q, block_rows(index)]
+        return pltpu.make_async_remote_copy(
+            src_ref=view, dst_ref=view, send_sem=send_sem.at[q, lane],
+            recv_sem=recv_sem.at[slot, q, index], device_id=target, device_id_type=MESH,
+        )
+
+    def lane_block(level, flipped_y, flipped_c):
+        yy = 1 - y if flipped_y else y
+        cc = 1 - c if flipped_c else c
+        return level * 4 + yy * 2 + cc
+
+    def head_sends(slot, q):
+        index = lane_block(first, False, False)
+        return (
+            (position == 1, send(slot, q, index, 1, to_b)),
+            (position <= 2, send(slot, q, index, 0, to_a)),
+            (None, send(slot, q, index, 2, to_y)),
+            (None, send(slot, q, index, 3, to_c)),
+        )
+
+    def tail_sends(slot, q):
+        index = lane_block(second, False, False)
+        return (
+            (position == 1, send(slot, q, index, 5, to_b)),
+            (position == 2, send(slot, q, index, 4, to_a)),
+            (None, send(slot, q, index, 6, to_y)),
+            (None, send(slot, q, index, 7, to_c)),
+        )
+
+    def across_sends(slot, q):
+        return (
+            send(slot, q, lane_block(first, True, False), 8, to_c),
+            send(slot, q, lane_block(second, True, False), 9, to_c),
+        )
+
+    def guarded(condition, action):
+        if condition is None:
+            action()
+        else:
+            pl.when(condition)(action)
+
+    def await_block(slot, q, index):
+        send(slot, q, index, 0, to_c).wait_recv()
+
+    def head(slot, q):
+        pl.when(not_owner)(lambda: await_block(slot, q, lane_block(first, False, False)))
+        for condition, copy in head_sends(slot, q):
+            guarded(condition, copy.start)
+
+    def tail(slot, q):
+        await_block(slot, q, lane_block(second, False, False))
+        for condition, copy in tail_sends(slot, q):
+            guarded(condition, copy.start)
+
+    def across(slot, q, which):
+        await_block(slot, q, lane_block((first, second)[which], True, False))
+        across_sends(slot, q)[which].start()
+
+    def collect(slot, q):
+        for flipped in (False, True):
+            for level in (first, second):
+                await_block(slot, q, lane_block(level, flipped, True))
+
+    def await_sends(slot, q):
+        for condition, copy in head_sends(slot, q) + tail_sends(slot, q):
+            guarded(condition, copy.wait_send)
+        for copy in across_sends(slot, q):
+            copy.wait_send()
+
+    def partial_copy(slot, q):
+        return pltpu.make_async_remote_copy(
+            src_ref=part.at[q], dst_ref=other.at[slot, q], send_sem=x_send.at[q],
+            recv_sem=x_recv.at[slot, q], device_id=to_x, device_id_type=MESH,
+        )
+
+    def final_copy(slot, q):
+        return pltpu.make_async_remote_copy(
+            src_ref=full.at[slot, q, block_rows(mine)], dst_ref=other.at[slot, q],
+            send_sem=x_send.at[q], recv_sem=x_recv.at[slot, q],
+            device_id=to_x, device_id_type=MESH,
+        )
+
+    def multiply(slot, q, source):
+        values = full[slot, source]
+        upper = values.astype(jnp.bfloat16)
+        split[:, :128] = upper
+        split[:, 128:] = (values - upper.astype(jnp.float32)).astype(jnp.bfloat16)
+        def image(which):
+            wide = jnp.dot(high_ref[q, which], split[...], preferred_element_type=jnp.float32)
+            rest = jnp.dot(low_ref[q, which], split[:, :128], preferred_element_type=jnp.float32)
+            return wide[:, :128] + (wide[:, 128:] + rest)
+        part[q] = image(0) + sign_row(-1.0, 1.0) * pltpu.roll(image(1), 64, 1)
+
+    def update(slot, q, weight, keep):
+        own = jnp.where(p == q, 1.0, 0.0)
+        centre = own * bounds_ref[0:1, :] + (1.0 - own) * partner_bounds[0:1, :]
+        spread = own * bounds_ref[1:2, :] + (1.0 - own) * partner_bounds[1:2, :]
+        current = full[slot, q, block_rows(mine), :]
+        previous = full[1 - slot, q, block_rows(mine), :]
+        image = part[q] + other[slot, q]
+        full[1 - slot, q, block_rows(mine), :] = (
+            weight * (image - centre * current) / spread - jnp.where(keep, previous, 0.0)
+        )
+
+    def step(k, carry):
+        slot = k % 2
+        later = k > 0
+        last = k == STEPS - 1
+        middle = k < STEPS - 1
+        head(slot, 0)
+        pl.when(later)(lambda: head(slot, 1))
+
+        @pl.when(jnp.logical_and(last, owner))
+        def _():
+            final_copy(slot, 0).start()
+            final_copy(slot, 1).start()
+
+        tail(slot, 0)
+        pl.when(later)(lambda: tail(slot, 1))
+        for which in (0, 1):
+            across(slot, 0, which)
+            pl.when(later)(functools.partial(across, slot, 1, which))
+        collect(slot, 0)
+        multiply(slot, 0, 0)
+        pl.when(jnp.logical_and(middle, not_owner))(lambda: partial_copy(slot, 0).start())
+        pl.when(later)(lambda: collect(slot, 1))
+        multiply(slot, 1, jnp.where(later, 1, 0))
+        await_sends(slot, 0)
+        pl.when(later)(lambda: await_sends(slot, 1))
+        pl.when(jnp.logical_and(middle, not_owner))(lambda: partial_copy(slot, 1).start())
+        odd = slot == 0
+        weight = jnp.where(odd, 1.0, 2.0)
+
+        @pl.when(jnp.logical_and(middle, owner))
+        def _():
+            for q in (0, 1):
+                partial_copy(slot, q).wait_recv()
+
+                @pl.when(k == 0)
+                def _():
+                    full[1, q, block_rows(mine), :] = jnp.zeros((rows, 128), jnp.float32)
+
+                update(slot, q, weight, slot == 1)
+
+        @pl.when(jnp.logical_and(middle, not_owner))
+        def _():
+            partial_copy(slot, 0).wait_send()
+            partial_copy(slot, 1).wait_send()
+
+        return carry
+
+    lax.fori_loop(0, STEPS, step, 0)
+    slot = (STEPS - 1) % 2
+
+    @pl.when(owner)
+    def _():
+        for q in (0, 1):
+            final_copy(slot, q).wait_send()
+            other[slot, q] = full[slot, q, block_rows(mine), :]
+
+    @pl.when(not_owner)
+    def _():
+        final_copy(slot, 0).wait_recv()
+        final_copy(slot, 1).wait_recv()
+
+    final_ref[...] = other[slot, p]
+
+    def gram(left, right):
+        whole = lax.dot_general(
+            left, right, (((0,), (0,)), ((), ())), precision=highest,
+            preferred_element_type=jnp.float32,
+        )
+        return whole[:64] + sign_row(1.0, -1.0) * pltpu.roll(whole[64:], 64, 1)
+
+    sums[5, 0] = gram(other[slot, 1 - p], part[1 - p])
+    cross = pltpu.make_async_remote_copy(
+        src_ref=sums.at[5, 0], dst_ref=arrived.at[4, 0], send_sem=g_send.at[4],
+        recv_sem=g_recv.at[4], device_id=to_x, device_id_type=MESH,
+    )
+    cross.start()
+    sums[0, 0] = gram(other[slot, p], other[slot, p])
+    own_projected = gram(other[slot, p], part[p])
+    cross.wait()
+    sums[0, 1] = own_projected + arrived[4, 0]
+    for stage, target in enumerate((to_c, to_y, to_a, to_b)):
+        copy = pltpu.make_async_remote_copy(
+            src_ref=sums.at[stage], dst_ref=arrived.at[stage], send_sem=g_send.at[stage],
+            recv_sem=g_recv.at[stage], device_id=target, device_id_type=MESH,
+        )
+        copy.start()
+        copy.wait()
+        sums[stage + 1] = sums[stage] + arrived[stage]
+    gram_ref[...] = sums[4]
+
+
+def filtered(bounds, start_vectors, high, low):
+    rows = start_vectors.shape[0]
+    points, _, _, cols = high.shape
+    vmem = pl.BlockSpec(memory_space=pltpu.VMEM)
+    dma = pltpu.SemaphoreType.DMA
+    return pl.pallas_call(
+        filter_kernel,
+        out_shape=(
+            jax.ShapeDtypeStruct((rows, 128), jnp.float32),
+            jax.ShapeDtypeStruct((2, 64, 128), jnp.float32),
+        ),
+        in_specs=[vmem] * 4,
+        out_specs=(vmem, vmem),
+        scratch_shapes=[
+            pltpu.VMEM((2, points, cols, 128), jnp.float32),
+            pltpu.VMEM((points, rows, 128), jnp.float32),
+            pltpu.VMEM((2, points, rows, 128), jnp.float32),
+            pltpu.VMEM((cols, 256), jnp.bfloat16),
+            pltpu.VMEM((8, 128), jnp.float32),
+            pltpu.VMEM((6, 2, 64, 128), jnp.float32),
+            pltpu.VMEM((5, 2, 64, 128), jnp.float32),
+            dma((points, 10)),
+            dma((2, points, 8)),
+            dma((points,)),
+            dma((2, points)),
+            dma((2,)),
+            dma((5,)),
+            dma((5,)),
+        ],
+        compiler_params=pltpu.CompilerParams(
+            collective_id=0, has_side_effects=True, vmem_limit_bytes=56 * 1024 * 1024
+        ),
+    )(bounds, start_vectors, high, low)
+
+
+def on_block(force_constants, offsets, qpoints, lower_bound, upper_bound, start_vectors):
+    cell_count = force_constants.shape[0]
+    qcount = qpoints.shape[0]
+    vector_count = start_vectors.shape[1] // 2
+    coefficients = phase_table(qpoints, offsets).reshape(2 * qcount, cell_count)
+    high, low = assemble(coefficients, force_constants, qcount)
+    centre = 0.5 * (upper_bound + lower_bound)
+    spread = 0.5 * (upper_bound - lower_bound)
+    bounds = jnp.broadcast_to(
+        jnp.concatenate([centre, spread, jnp.zeros((6,), jnp.float32)])[:, None], (8, 128)
+    )
+    final_pass, grams = filtered(bounds, start_vectors, high, low)
+    over_real, over_imag = grams[0, :, :vector_count], grams[0, :, vector_count:]
+    proj_real, proj_imag = grams[1, :, :vector_count], grams[1, :, vector_count:]
+    inverse_real, inverse_imag = factor_inverse(over_real, over_imag)
+    basis_local = math.sqrt(MODES) * product(final_pass, right_block(inverse_real, inverse_imag))
+    temp_real, temp_imag = complex_times(proj_real, proj_imag, inverse_real.T, -inverse_imag.T)
+    ritz_real, ritz_imag = complex_times(inverse_real, inverse_imag, temp_real, temp_imag)
+    ritz_local = jnp.concatenate([ritz_real, ritz_imag], axis=1)
+    return (basis_local[None], ritz_local[None])
+
+
 def solution(mesh):
+    paired = mesh.shape["pb"] == 2 and mesh.shape["row"] == 16
     return jax.shard_map(
-        on_device,
+        on_block if paired else on_device,
         mesh=mesh,
         in_specs=(P(None, "row", "pb"), P(), P(), P("pb"), P("pb"), P("row", None)),
         out_specs=(P("pb", "row", None), P("pb", None, None)),

time: 607 us -> 234 us (0.39); the launches traced: 598 us -> 233 us
  waiting for transfers between devices: 367 us -> 0 us
  Pallas kernels: 0 us -> 192 us
  matrix products: 129 us -> 3 us
  local copies, waits for them, and re-layouts: 48.1 us -> 10 us
  between operations: 16.1 us -> 2.14 us
  starting transfers between devices: 8.98 us -> 0 us
    pallas_call x0 -> x2, Pallas kernels: none -> 192 us  [the longest x1 173 us: filtered(): pl.pallas_call(filter_kernel, out_shape=(jax.ShapeDtypeStruct((rows, 128)...]
    all_gather x5 -> x0, waiting for transfers between devices: 163 us -> none  [apply_matrix(): return accumulate(lax.all_gather(vectors, 'row', axis=0, tiled=True))]
    dot_general x20 -> x9, matrix products: 125 us -> 2.73 us  [product(): jnp.dot(left, right, precision=highest, preferred_element_type=jnp.float32)]
    all_to_all x1 -> x0, waiting for transfers between devices: 115 us -> none  [on_device(): lax.all_to_all(partial_value, 'pb', split_axis=0, concat_axis=3, tiled=True)]
    psum x1 -> x0, waiting for transfers between devices: 87.1 us -> none  [on_device(): lax.psum((inner_product(final_pass, final_pass), inner_product(final_pass...]
    all_to_all x2 -> x0, local copies, waits for them, and re-layouts: 30.3 us -> none  [on_device(): lax.all_to_all(partial_value, 'pb', split_axis=0, concat_axis=3, tiled=True)]
    dot_general x1 -> x0, local copies, waits for them, and re-layouts: 9.7 us -> none  [product(): jnp.dot(left, right, precision=highest, preferred_element_type=jnp.float32)]
    all_to_all x1 -> x0, starting transfers between devices: 7.75 us -> none  [on_device(): lax.all_to_all(partial_value, 'pb', split_axis=0, concat_axis=3, tiled=True)]
  transfers between devices with their start and end apart: 7 -> 0, of which waited for: 6 -> 0; matrix products, arithmetic and copies ran while one was open for 3% -> 0% of each run, Pallas kernels for 0% -> 0%
where the time goes in v1:
time: 234 us; the launch traced here: 233 us
  Pallas kernels  192 us (82%)
  other arithmetic  25.4 us (11%)
  local copies, waits for them, and re-layouts  10 us (4%)
  matrix products  3 us (1%)
    pallas_call x1, Pallas kernels, filtered(): pl.pallas_call(filter_kernel, out_shape=(jax.ShapeDtypeStruct((rows, 128)...  173 us
    pallas_call x1, Pallas kernels, assemble(): pl.pallas_call(assemble_kernel, grid=(rows // tile,), out_shape=(shape, s...  19.8 us
    another operation x4, other arithmetic, factor_inverse(): lower_factor = jnp.linalg.cholesky(embedded)  12.5 us
    another operation x3, other arithmetic, factor_inverse(): jax.scipy.linalg.solve_triangular(lower_factor, identity, lower=True)  10.5 us

profile of v1, /device:TPU:0, one launch (start us, length us, event | category | flops | bytes accessed | tf_op | source)
XLA Modules:
  0.0 233.0 jit_solution(3601713462481489432)
XLA Ops:
  1.9 0.1 pad_maximum_fusion.2
  2.0 0.7 broadcast_in_dim.8.bounds_ref
  2.7 0.8 copy.20
  3.4 0.8 multiply_reduce_fusion
  4.2 0.1 fusion.42
  4.3 0.6 copy.21
  4.9 19.8 %shard_map.77 = (bf16[2,2,288,2304]{3,2,1,0:T(8,128)(2,1)}, bf16[2,2,288,2304]{3,2,1,0:T(8,128)(2,1)}) custom-call(f32[4,9]{1,0:T(4,128)} %bitcast.75, f32[9,288,2304]{2,1,0:T(8,128)} %force_ref.1), custom_call_target="tpu_custom_call" | custom-call | tf_op jit(solution)/shard_map/pallas_call | solution.py:159
  24.6 172.6 %shard_map.78 = (f32[288,128]{1,0:T(8,128)}, f32[2,64,128]{2,1,0:T(8,128)}) custom-call(f32[8,128]{1,0:T(8,128)} %broadcast_in_dim.8.bounds_ref, f32[288,128]{1,0:T(8,128)} %start_ref.1, bf16[2,2,288,2304]{3,2,1,0:T(8,128)(2,1)} %get-tuple-element.6.high_ref, bf16[2,2,288,2304]{3,2,1,0:T(8,128)(2,1)} %get-tuple-element.7.low_ref), custom_call_target="tpu_custom_call" | custom-call | tf_op jit(solution)/shard_map/pallas_call | solution.py:421
  197.3 0.0 copy-start
  197.3 0.9 slice_bitcast_fusion
  198.2 0.8 fusion.45
  199.1 0.0 copy-start.1
  199.1 2.7 %copy.22 = f32[64,2,64,2]{3,2,1,0:T(8,128)} copy(f32[64,2,64,2]{2,0,3,1:T(8,128)S(1)} %pad_maximum_fusion) | data formatting | bytes 131072 | tf_op jit(solution)/shard_map/stack | solution.py:44
  201.8 4.0 %reshape.123 = f32[128,128]{1,0:T(8,128)S(1)} reshape(f32[64,2,64,2]{3,2,1,0:T(8,128)} %copy.22) | data formatting | bytes 131072 | tf_op jit(solution)/shard_map/reshape | solution.py:47
  205.8 0.1 copy.23
  205.9 11.7 %cholesky.18 = f32[128,128]{1,0:T(8,128)S(1)} custom-call(f32[128,128]{1,0:T(8,128)S(1)} %fusion.11), custom_call_target="Cholesky" | custom-call | tf_op jit(solution)/shard_map/jit(cholesky)/cholesky | solution.py:48
  217.7 0.6 compare_reduce_fusion
  218.3 0.7 fusion.1
  219.0 9.8 %custom-call.7 = f32[1,128,128]{1,2,0:T(8,128)S(1)} custom-call(f32[1,128,128]{2,1,0:T(8,128)S(1)} %fusion.1), custom_call_target="InvertDiagBlocksLowerTriangular" | custom-call | tf_op jit(solution)/shard_map/jit(_solve_triangular)/triangular_solve | solution.py:50
  228.8 0.1 copy.24
  228.9 0.1 triangular_solve.56
  229.1 0.1 iota_compare_fusion
  229.2 0.3 fusion.9
  229.5 0.0 copy-done
  229.5 0.2 fusion.18
  229.6 0.2 convolution_subtract_fusion.1
  229.9 0.2 fusion.23
  230.1 0.2 fusion.16
  230.3 0.2 convolution_add_fusion.1
  230.5 0.2 convolution_subtract_fusion
  230.8 0.2 fusion.26
  231.0 0.2 convolution_add_fusion
  231.2 0.7 maximum_bitcast_fusion.2
  232.0 0.0 copy-done.1
  232.0 1.0 fusion
  (10 shorter events, 0.1 us)
Async XLA Ops:
  197.3 32.2 %copy-start = (f32[2,64,128]{2,1,0:T(8,128)S(1)}, f32[2,64,128]{2,1,0:T(8,128)}, u32[]{:S(2)}) copy-start(f32[2,64,128]{2,1,0:T(8,128)} %get-tuple-element.9) | copy-start | bytes 196612
  199.1 32.9 %copy-start.1 = (f32[288,128]{1,0:T(8,128)S(1)}, f32[288,128]{1,0:T(8,128)}, u32[]{:S(2)}) copy-start(f32[288,128]{1,0:T(8,128)} %get-tuple-element.8) | copy-start | bytes 442372

commit v2 on v1

--- a/solution.py
+++ b/solution.py
@@ -153,7 +153,7 @@
 
 def assemble(coefficients, force_constants, points):
     cells, rows, cols = force_constants.shape
-    tile = 16
+    tile = 48
     shape = jax.ShapeDtypeStruct((points, 2, rows, cols), jnp.bfloat16)
     block = pl.BlockSpec((points, 2, tile, cols), lambda i: (0, 0, i, 0))
     return pl.pallas_call(
@@ -448,10 +448,65 @@
     )(bounds, start_vectors, high, low)
 
 
+def finish_kernel(scale, final_ref, gram_ref, basis_ref, ritz_ref):
+    size = gram_ref.shape[1]
+    tile = 8
+    gram = [gram_ref[0, t * tile:(t + 1) * tile, :] for t in range(size // tile)]
+    lane = lax.broadcasted_iota(jnp.int32, (tile, 128), 1)
+    line = lax.broadcasted_iota(jnp.int32, (tile, 128), 0)
+    inverse = [jnp.where(lane == line + t * tile, 1.0, 0.0) for t in range(size // tile)]
+    turn = sign_row(-1.0, 1.0)
+    for j in range(size):
+        home, at = j // tile, j % tile
+        row = gram[home][at:at + 1, :]
+        pivot = row[:, j:j + 1]
+        row = row / pivot
+        mate = inverse[home][at:at + 1, :] / pivot
+        row_turned = turn * pltpu.roll(row, 64, 1)
+        mate_turned = turn * pltpu.roll(mate, 64, 1)
+        for t in range(home, size // tile):
+            real = gram[t][:, j:j + 1]
+            imag = gram[t][:, 64 + j:65 + j]
+            if t == home:
+                below = line[:, :1] > at
+                real = jnp.where(below, real, 0.0)
+                imag = jnp.where(below, imag, 0.0)
+            gram[t] = gram[t] - (real * row + imag * row_turned)
+            inverse[t] = inverse[t] - (real * mate + imag * mate_turned)
+    scaled = []
+    for t in range(size // tile):
+        diagonal = jnp.sum(jnp.where(lane == line + t * tile, gram[t], 0.0), axis=1, keepdims=True)
+        scaled.append(inverse[t] / jnp.sqrt(diagonal))
+    whole = jnp.concatenate(scaled, axis=0)
+    paired = jnp.concatenate([whole, turn * pltpu.roll(whole, 64, 1)], axis=0)
+
+    def against(left):
+        return lax.dot_general(
+            left, paired, (((1,), (1,)), ((), ())), precision=highest,
+            preferred_element_type=jnp.float32,
+        )
+
+    basis_ref[...] = scale * against(final_ref[...])
+    half = against(gram_ref[1])
+    ritz_ref[...] = product(whole, jnp.concatenate([half, turn * pltpu.roll(half, 64, 1)], axis=0))
+
+
+def finish(final_pass, grams, modes):
+    vmem = pl.BlockSpec(memory_space=pltpu.VMEM)
+    return pl.pallas_call(
+        functools.partial(finish_kernel, math.sqrt(modes)),
+        out_shape=(
+            jax.ShapeDtypeStruct(final_pass.shape, jnp.float32),
+            jax.ShapeDtypeStruct(grams.shape[1:], jnp.float32),
+        ),
+        in_specs=[vmem] * 2,
+        out_specs=(vmem, vmem),
+    )(final_pass, grams)
+
+
 def on_block(force_constants, offsets, qpoints, lower_bound, upper_bound, start_vectors):
     cell_count = force_constants.shape[0]
     qcount = qpoints.shape[0]
-    vector_count = start_vectors.shape[1] // 2
     coefficients = phase_table(qpoints, offsets).reshape(2 * qcount, cell_count)
     high, low = assemble(coefficients, force_constants, qcount)
     centre = 0.5 * (upper_bound + lower_bound)
@@ -460,13 +515,7 @@
         jnp.concatenate([centre, spread, jnp.zeros((6,), jnp.float32)])[:, None], (8, 128)
     )
     final_pass, grams = filtered(bounds, start_vectors, high, low)
-    over_real, over_imag = grams[0, :, :vector_count], grams[0, :, vector_count:]
-    proj_real, proj_imag = grams[1, :, :vector_count], grams[1, :, vector_count:]
-    inverse_real, inverse_imag = factor_inverse(over_real, over_imag)
-    basis_local = math.sqrt(MODES) * product(final_pass, right_block(inverse_real, inverse_imag))
-    temp_real, temp_imag = complex_times(proj_real, proj_imag, inverse_real.T, -inverse_imag.T)
-    ritz_real, ritz_imag = complex_times(inverse_real, inverse_imag, temp_real, temp_imag)
-    ritz_local = jnp.concatenate([ritz_real, ritz_imag], axis=1)
+    basis_local, ritz_local = finish(final_pass, grams, MODES)
     return (basis_local[None], ritz_local[None])
 
 

time: 234 us -> 204 us (0.87)
  other arithmetic: 25.4 us -> 0.9 us
  local copies, waits for them, and re-layouts: 10 us -> 2.01 us
  Pallas kernels: 192 us -> 199 us
  matrix products: 3 us -> 0 us
    another operation x9 -> x0, other arithmetic: 23 us -> none  [the longest x4 12.5 us: factor_inverse(): lower_factor = jnp.linalg.cholesky(embedded)]
    pallas_call x0 -> x1, Pallas kernels: none -> 12.1 us  [finish(): pl.pallas_call(functools.partial(finish_kernel, math.sqrt(modes)), out_sh...]
    pallas_call x1, Pallas kernels: 19.8 us -> 14.3 us  [assemble(): pl.pallas_call(assemble_kernel, grid=(rows // tile,), out_shape=(shape, s...]
    reshape x2 -> x0, local copies, waits for them, and re-layouts: 4.09 us -> none  [factor_inverse(): embedded = jnp.stack([jnp.stack([gram_real, -gram_imag], axis=2), jnp.sta...]
    another operation x5 -> x1, local copies, waits for them, and re-layouts: 2.96 us -> 0.01 us  [the longest x1 2.71 us: factor_inverse(): jnp.stack([jnp.stack([gram_real, -gram_imag], axis=2), jnp.stack([gram_im...]
    dot_general x9 -> x0, matrix products: 2.73 us -> none  [product(): jnp.dot(left, right, precision=highest, preferred_element_type=jnp.float32)]
where the time goes in v2:
time: 204 us
  Pallas kernels  199 us (98%)
    pallas_call x1, Pallas kernels, filtered(): pl.pallas_call(filter_kernel, out_shape=(jax.ShapeDtypeStruct((rows, 128)...  172 us
    pallas_call x1, Pallas kernels, assemble(): pl.pallas_call(assemble_kernel, grid=(rows // tile,), out_shape=(shape, s...  14.3 us
    pallas_call x1, Pallas kernels, finish(): pl.pallas_call(functools.partial(finish_kernel, math.sqrt(modes)), out_sh...  12.1 us

profile of v2, /device:TPU:0, one launch (start us, length us, event | category | flops | bytes accessed | tf_op | source)
XLA Modules:
  0.0 203.8 jit_solution(10808516015838230972)
XLA Ops:
  1.9 0.1 pad_maximum_fusion.1
  2.0 0.8 copy.10
  2.8 0.8 multiply_reduce_fusion
  3.5 0.1 fusion.4
  3.6 0.6 copy.11
  4.2 0.7 broadcast_in_dim.6.bounds_ref
  4.9 14.3 %shard_map.77 = (bf16[2,2,288,2304]{3,2,1,0:T(8,128)(2,1)}, bf16[2,2,288,2304]{3,2,1,0:T(8,128)(2,1)}) custom-call(f32[4,9]{1,0:T(4,128)} %bitcast.9, f32[9,288,2304]{2,1,0:T(8,128)} %force_ref.1), custom_call_target="tpu_custom_call" | custom-call | tf_op jit(solution)/shard_map/pallas_call | solution.py:159
  19.2 172.4 %shard_map.78 = (f32[288,128]{1,0:T(8,128)}, f32[2,64,128]{2,1,0:T(8,128)}) custom-call(f32[8,128]{1,0:T(8,128)} %broadcast_in_dim.6.bounds_ref, f32[288,128]{1,0:T(8,128)} %start_ref.1, bf16[2,2,288,2304]{3,2,1,0:T(8,128)(2,1)} %get-tuple-element.8.high_ref, bf16[2,2,288,2304]{3,2,1,0:T(8,128)(2,1)} %get-tuple-element.9.low_ref), custom_call_target="tpu_custom_call" | custom-call | tf_op jit(solution)/shard_map/pallas_call | solution.py:421
  191.6 12.1 %shard_map.79 = (f32[288,128]{1,0:T(8,128)}, f32[64,128]{1,0:T(8,128)}) custom-call(f32[288,128]{1,0:T(8,128)} %get-tuple-element.10.final_ref, f32[2,64,128]{2,1,0:T(8,128)} %get-tuple-element.11.gram_ref), custom_call_target="tpu_custom_call" | custom-call | tf_op jit(solution)/shard_map/pallas_call | solution.py:496
  (2 shorter events, 0.0 us)

commit v3 on v2

--- a/solution.py
+++ b/solution.py
@@ -124,6 +124,7 @@
 
 
 STEPS = 5
+PIECES = 2
 MESH = pl.DeviceIdType.MESH
 
 
@@ -217,11 +218,14 @@
 
     bound_copy.wait()
 
-    def send(slot, q, index, lane, target):
-        view = full.at[slot, q, block_rows(index)]
+    depth = rows // PIECES
+
+    def send(slot, q, index, piece, lane, target):
+        where = pl.ds(pl.multiple_of(index * rows + piece * depth, 8), depth)
+        view = full.at[slot, q, where]
         return pltpu.make_async_remote_copy(
-            src_ref=view, dst_ref=view, send_sem=send_sem.at[q, lane],
-            recv_sem=recv_sem.at[slot, q, index], device_id=target, device_id_type=MESH,
+            src_ref=view, dst_ref=view, send_sem=send_sem.at[q, lane, piece],
+            recv_sem=recv_sem.at[slot, q, index, piece], device_id=target, device_id_type=MESH,
         )
 
     def lane_block(level, flipped_y, flipped_c):
@@ -229,29 +233,27 @@
         cc = 1 - c if flipped_c else c
         return level * 4 + yy * 2 + cc
 
-    def head_sends(slot, q):
+    def head_sends(slot, q, piece):
         index = lane_block(first, False, False)
         return (
-            (position == 1, send(slot, q, index, 1, to_b)),
-            (position <= 2, send(slot, q, index, 0, to_a)),
-            (None, send(slot, q, index, 2, to_y)),
-            (None, send(slot, q, index, 3, to_c)),
-        )
-
-    def tail_sends(slot, q):
+            (position == 1, send(slot, q, index, piece, 1, to_b)),
+            (position <= 2, send(slot, q, index, piece, 0, to_a)),
+            (None, send(slot, q, index, piece, 2, to_y)),
+            (None, send(slot, q, index, piece, 3, to_c)),
+        )
+
+    def tail_sends(slot, q, piece):
         index = lane_block(second, False, False)
         return (
-            (position == 1, send(slot, q, index, 5, to_b)),
-            (position == 2, send(slot, q, index, 4, to_a)),
-            (None, send(slot, q, index, 6, to_y)),
-            (None, send(slot, q, index, 7, to_c)),
-        )
-
-    def across_sends(slot, q):
-        return (
-            send(slot, q, lane_block(first, True, False), 8, to_c),
-            send(slot, q, lane_block(second, True, False), 9, to_c),
-        )
+            (position == 1, send(slot, q, index, piece, 5, to_b)),
+            (position == 2, send(slot, q, index, piece, 4, to_a)),
+            (None, send(slot, q, index, piece, 6, to_y)),
+            (None, send(slot, q, index, piece, 7, to_c)),
+        )
+
+    def across_send(slot, q, piece, which):
+        index = lane_block((first, second)[which], True, False)
+        return send(slot, q, index, piece, 8 + which, to_c)
 
     def guarded(condition, action):
         if condition is None:
@@ -259,33 +261,44 @@
         else:
             pl.when(condition)(action)
 
-    def await_block(slot, q, index):
-        send(slot, q, index, 0, to_c).wait_recv()
-
-    def head(slot, q):
-        pl.when(not_owner)(lambda: await_block(slot, q, lane_block(first, False, False)))
-        for condition, copy in head_sends(slot, q):
-            guarded(condition, copy.start)
+    def await_block(slot, q, index, piece):
+        send(slot, q, index, piece, 0, to_c).wait_recv()
+
+    def head(slot, q, relay):
+        for piece in range(PIECES):
+            if relay:
+                await_block(slot, q, lane_block(first, False, False), piece)
+            for condition, copy in head_sends(slot, q, piece):
+                guarded(condition, copy.start)
 
     def tail(slot, q):
-        await_block(slot, q, lane_block(second, False, False))
-        for condition, copy in tail_sends(slot, q):
-            guarded(condition, copy.start)
-
-    def across(slot, q, which):
-        await_block(slot, q, lane_block((first, second)[which], True, False))
-        across_sends(slot, q)[which].start()
+        for piece in range(PIECES):
+            await_block(slot, q, lane_block(second, False, False), piece)
+            for condition, copy in tail_sends(slot, q, piece):
+                guarded(condition, copy.start)
+
+    def across(slot, q):
+        for which in (0, 1):
+            for piece in range(PIECES):
+                await_block(slot, q, lane_block((first, second)[which], True, False), piece)
+                across_send(slot, q, piece, which).start()
 
     def collect(slot, q):
         for flipped in (False, True):
             for level in (first, second):
-                await_block(slot, q, lane_block(level, flipped, True))
+                for piece in range(PIECES):
+                    await_block(slot, q, lane_block(level, flipped, True), piece)
+
+    def gathered(slot, q):
+        across(slot, q)
+        collect(slot, q)
 
     def await_sends(slot, q):
-        for condition, copy in head_sends(slot, q) + tail_sends(slot, q):
-            guarded(condition, copy.wait_send)
-        for copy in across_sends(slot, q):
-            copy.wait_send()
+        for piece in range(PIECES):
+            for condition, copy in head_sends(slot, q, piece) + tail_sends(slot, q, piece):
+                guarded(condition, copy.wait_send)
+            for which in (0, 1):
+                across_send(slot, q, piece, which).wait_send()
 
     def partial_copy(slot, q):
         return pltpu.make_async_remote_copy(
@@ -300,11 +313,13 @@
             device_id=to_x, device_id_type=MESH,
         )
 
-    def multiply(slot, q, source):
-        values = full[slot, source]
+    def divide(slot, q):
+        values = full[slot, q]
         upper = values.astype(jnp.bfloat16)
         split[:, :128] = upper
         split[:, 128:] = (values - upper.astype(jnp.float32)).astype(jnp.bfloat16)
+
+    def multiply(q):
         def image(which):
             wide = jnp.dot(high_ref[q, which], split[...], preferred_element_type=jnp.float32)
             rest = jnp.dot(low_ref[q, which], split[:, :128], preferred_element_type=jnp.float32)
@@ -325,35 +340,34 @@
     def step(k, carry):
         slot = k % 2
         later = k > 0
-        last = k == STEPS - 1
         middle = k < STEPS - 1
-        head(slot, 0)
-        pl.when(later)(lambda: head(slot, 1))
-
-        @pl.when(jnp.logical_and(last, owner))
-        def _():
-            final_copy(slot, 0).start()
-            final_copy(slot, 1).start()
-
-        tail(slot, 0)
-        pl.when(later)(lambda: tail(slot, 1))
-        for which in (0, 1):
-            across(slot, 0, which)
-            pl.when(later)(functools.partial(across, slot, 1, which))
-        collect(slot, 0)
-        multiply(slot, 0, 0)
-        pl.when(jnp.logical_and(middle, not_owner))(lambda: partial_copy(slot, 0).start())
-        pl.when(later)(lambda: collect(slot, 1))
-        multiply(slot, 1, jnp.where(later, 1, 0))
-        await_sends(slot, 0)
-        pl.when(later)(lambda: await_sends(slot, 1))
-        pl.when(jnp.logical_and(middle, not_owner))(lambda: partial_copy(slot, 1).start())
-        odd = slot == 0
-        weight = jnp.where(odd, 1.0, 2.0)
-
-        @pl.when(jnp.logical_and(middle, owner))
-        def _():
-            for q in (0, 1):
+        weight = jnp.where(slot == 0, 1.0, 2.0)
+        for q in (0, 1):
+            if q == 0:
+                gathered(slot, q)
+                divide(slot, q)
+            else:
+                @pl.when(later)
+                def _():
+                    gathered(slot, q)
+                    divide(slot, q)
+
+            @pl.when(jnp.logical_and(later, not_owner))
+            def _():
+                partial_copy(1 - slot, q).wait_send()
+
+            multiply(q)
+            guarded(None if q == 0 else later, functools.partial(await_sends, slot, q))
+            pl.when(jnp.logical_and(middle, not_owner))(partial_copy(slot, q).start)
+
+            other_slot, other_q, ready = (slot, 1, later) if q == 0 else (1 - slot, 0, middle)
+            pl.when(jnp.logical_and(ready, not_owner))(
+                functools.partial(head, other_slot, other_q, True)
+            )
+            pl.when(ready)(functools.partial(tail, other_slot, other_q))
+
+            @pl.when(jnp.logical_and(middle, owner))
+            def _():
                 partial_copy(slot, q).wait_recv()
 
                 @pl.when(k == 0)
@@ -361,14 +375,17 @@
                     full[1, q, block_rows(mine), :] = jnp.zeros((rows, 128), jnp.float32)
 
                 update(slot, q, weight, slot == 1)
-
-        @pl.when(jnp.logical_and(middle, not_owner))
-        def _():
-            partial_copy(slot, 0).wait_send()
-            partial_copy(slot, 1).wait_send()
+                head(1 - slot, q, False)
+
+                @pl.when(k == STEPS - 2)
+                def _():
+                    final_copy(1 - slot, q).start()
 
         return carry
 
+    pl.when(owner)(functools.partial(head, 0, 0, False))
+    pl.when(not_owner)(functools.partial(head, 0, 0, True))
+    tail(0, 0)
     lax.fori_loop(0, STEPS, step, 0)
     slot = (STEPS - 1) % 2
 
@@ -434,8 +451,8 @@
             pltpu.VMEM((8, 128), jnp.float32),
             pltpu.VMEM((6, 2, 64, 128), jnp.float32),
             pltpu.VMEM((5, 2, 64, 128), jnp.float32),
-            dma((points, 10)),
-            dma((2, points, 8)),
+            dma((points, 10, PIECES)),
+            dma((2, points, 8, PIECES)),
             dma((points,)),
             dma((2, points)),
             dma((2,)),

time: 204 us -> 180 us (0.88)
  Pallas kernels: 199 us -> 175 us
    pallas_call x1, Pallas kernels: 172 us -> 148 us  [filtered(): pl.pallas_call(filter_kernel, out_shape=(jax.ShapeDtypeStruct((rows, 128)...]
where the time goes in v3:
time: 180 us; the launch traced here: 179 us
  Pallas kernels  175 us (97%)
  local copies, waits for them, and re-layouts  2.01 us (1%)
  between operations  1.95 us (1%)
    pallas_call x1, Pallas kernels, filtered(): pl.pallas_call(filter_kernel, out_shape=(jax.ShapeDtypeStruct((rows, 128)...  148 us
    pallas_call x1, Pallas kernels, assemble(): pl.pallas_call(assemble_kernel, grid=(rows // tile,), out_shape=(shape, s...  14.3 us
    pallas_call x1, Pallas kernels, finish(): pl.pallas_call(functools.partial(finish_kernel, math.sqrt(modes)), out_sh...  12.1 us

profile of v3, /device:TPU:0, one launch (start us, length us, event | category | flops | bytes accessed | tf_op | source)
XLA Modules:
  0.0 179.4 jit_solution(10106848356669282069)
XLA Ops:
  1.9 0.1 pad_maximum_fusion.1
  2.0 0.8 copy.10
  2.8 0.8 multiply_reduce_fusion
  3.5 0.1 fusion.4
  3.6 0.6 copy.11
  4.2 0.7 broadcast_in_dim.6.bounds_ref
  4.9 14.3 %shard_map.77 = (bf16[2,2,288,2304]{3,2,1,0:T(8,128)(2,1)}, bf16[2,2,288,2304]{3,2,1,0:T(8,128)(2,1)}) custom-call(f32[4,9]{1,0:T(4,128)} %bitcast.9, f32[9,288,2304]{2,1,0:T(8,128)} %force_ref.1), custom_call_target="tpu_custom_call" | custom-call | tf_op jit(solution)/shard_map/pallas_call | solution.py:160
  19.2 148.0 %shard_map.78 = (f32[288,128]{1,0:T(8,128)}, f32[2,64,128]{2,1,0:T(8,128)}) custom-call(f32[8,128]{1,0:T(8,128)} %broadcast_in_dim.6.bounds_ref, f32[288,128]{1,0:T(8,128)} %start_ref.1, bf16[2,2,288,2304]{3,2,1,0:T(8,128)(2,1)} %get-tuple-element.8.high_ref, bf16[2,2,288,2304]{3,2,1,0:T(8,128)(2,1)} %get-tuple-element.9.low_ref), custom_call_target="tpu_custom_call" | custom-call | tf_op jit(solution)/shard_map/pallas_call | solution.py:438
  167.3 12.1 %shard_map.79 = (f32[288,128]{1,0:T(8,128)}, f32[64,128]{1,0:T(8,128)}) custom-call(f32[288,128]{1,0:T(8,128)} %get-tuple-element.10.final_ref, f32[2,64,128]{2,1,0:T(8,128)} %get-tuple-element.11.gram_ref), custom_call_target="tpu_custom_call" | custom-call | tf_op jit(solution)/shard_map/pallas_call | solution.py:513
  (2 shorter events, 0.0 us)
